TPU v7x, 256 devices: a whole 4x4x8 slice. The times are simulated.
256 devices in a mesh: wide: 32 (over x, y, core), narrow: 8 (over z).
Axes of the slice: x: 4, y: 4, z: 8, core: 2. Of those that a mesh axis runs over, the one named last changes fastest.
Arguments:
- decode_hidden_input: bfloat16 [1024, 8192], P('wide'), may hold values from -6 to 6
- queries: bfloat16 [1024, 8192], P('wide', 'narrow'), may hold values from -8 to 8
- cached_key_rows: bfloat16 [1024, 256, 1024], P('wide', None, 'narrow'), may hold values from -4 to 4
- cached_value_rows: bfloat16 [1024, 256, 1024], P('wide', None, 'narrow'), may hold values from -6 to 6
- lengths: int32 [1024], P('wide'), may hold values from 2 to 256, as said below
- decode_adapter_index: int32 [1024], P('wide'), may hold values from 0 to 511, as said below
- key_matrix: bfloat16 [8192, 1024], P(None, 'narrow'), may hold values from -0.0625 to 0.0625
- value_matrix: bfloat16 [8192, 1024], P(None, 'narrow'), may hold values from -0.0625 to 0.0625
- adapter_down_map: bfloat16 [512, 16, 8192], P('wide', None, 'narrow'), may hold values from -0.0625 to 0.0625
- adapter_up_map: bfloat16 [512, 16, 1024], P('wide', None, 'narrow'), may hold values from -0.1875 to 0.1875
- training_hidden_input: bfloat16 [32768, 8192], P('wide', 'narrow'), may hold values from -6 to 6
- cotangent: bfloat16 [32768, 1024], P('wide', 'narrow'), may hold values from -0.3984375 to 0.3984375
- training_adapter_index: int32 [32768], P('wide'), may hold values from 0 to 511, as said below
- rewards: int32 [32768], P('wide'), may hold values from -2 to 2
Outputs:
- attended: bfloat16 [1024, 8192], P('wide', 'narrow')
- fresh_values: bfloat16 [1024, 1024], P('wide', 'narrow')
- grad_down: float32 [512, 16, 8192], P('wide', None, 'narrow')
- grad_up: float32 [512, 16, 1024], P('wide', None, 'narrow')
Inputs may be any that keep to these rules, and one draw needn't show every extreme that they name: `decode_adapter_index`: of the 32 rows of one index of wide, at most 2 use adapters of one owner (adapters o * 16 to (o + 1) * 16 - 1); in every draw one owner gets exactly 2 rows from every index of wide. `training_adapter_index`: of the 1024 tokens of one index of wide, at most 64 use adapters of one owner (adapters o * 16 to (o + 1) * 16 - 1); in every draw one owner gets exactly 64 tokens from every index of wide. `lengths`: every block of 32 rows holds a row of length 256.
All inputs are finite; a program needn't handle non-finite values.
Results may differ from a plain program's by a relative error of at most 0.0051.
Values may be sent and summed in bfloat16 or wider, within the bound.
A program may use at most 64 MiB of HBM per device.

v0:
```python
import math

import jax
import jax.numpy as jnp
from jax import lax
from jax.sharding import PartitionSpec as P

HEADS = 64
KEY_VALUE_HEADS = 8
HEAD_SIZE = 128
CACHE = 256


ADAPTER_SCALE = 2.0
NEG_FILL = -1e30


def copy_for_each(shard, axis):
    devices = lax.axis_size(axis)
    return lax.all_to_all(
        jnp.broadcast_to(shard[None], (devices, *shard.shape)), axis, 0, 0, tiled=True
    )


def taken_together(shard, axis):
    everything = copy_for_each(shard, axis)
    return jnp.sum(everything, axis=0)


def side_by_side(arrays, axis, split_dim, concat_dim, along):
    both = jnp.concatenate(arrays, axis=along)
    out, at, gathered = (
        lax.all_to_all(both, axis, split_axis=split_dim, concat_axis=concat_dim, tiled=True),
        0,
        [],
    )
    for a in arrays:
        gathered.append(lax.slice_in_dim(out, at, at + a.shape[along], axis=along))
        at += a.shape[along]
    return tuple(gathered)


def over_pieces(shard, axis):
    return lax.all_gather(shard, axis).sum(0)


def pack_slots(adapter_ids, owners, owner_totals, capacity):
    owner_of = adapter_ids // owner_totals
    owner_match = (owner_of[:, None] == jnp.arange(owners, dtype=jnp.int32)[None, :]).astype(
        jnp.int32
    )
    earlier = jnp.cumsum(owner_match, axis=0) - owner_match
    position = jnp.sum(earlier * owner_match, axis=1)
    target = owner_of * capacity + position
    return jnp.arange(owners * capacity, dtype=jnp.int32)[:, None] == target[None, :]


def place_rows(slot_match, data, owners):
    placed = jnp.dot(
        slot_match.astype(jnp.bfloat16), data, preferred_element_type=jnp.float32
    ).astype(jnp.bfloat16)
    return placed.reshape(owners, -1, data.shape[1])


def place_codes(slot_match, values, owners):
    return jnp.sum(slot_match.astype(jnp.int32) * values[None, :], axis=1).reshape(owners, -1)


def code_match(codes, owner_totals):
    return codes[:, None] == jnp.arange(1, owner_totals + 1, dtype=jnp.int32)[None, :]


def pick_rank(codes, products, owner_totals):
    slot_count = codes.shape[0]
    chosen = code_match(codes, owner_totals).astype(jnp.float32)
    return jnp.sum(products.reshape(slot_count, owner_totals, -1) * chosen[:, :, None], axis=1)


def spread_rank(codes, factors, owner_totals):
    slot_count = codes.shape[0]
    chosen = code_match(codes, owner_totals).astype(jnp.bfloat16)
    return (chosen[:, :, None] * factors[:, None, :]).reshape(slot_count, -1)


def accumulate(codes, input_rows, incoming_gradient, scaled_rank, scaled_back, owner_totals):
    spread_back = spread_rank(codes, scaled_back, owner_totals)
    grad_down = jnp.einsum("sa,sd->ad", spread_back, input_rows, preferred_element_type=jnp.float32)
    spread_hidden = spread_rank(codes, scaled_rank, owner_totals)
    grad_up = jnp.einsum(
        "sa,sk->ak", spread_hidden, incoming_gradient, preferred_element_type=jnp.float32
    )
    return (
        grad_down.reshape(owner_totals, -1, input_rows.shape[1]),
        grad_up.reshape(owner_totals, -1, incoming_gradient.shape[1]),
    )


def owner_delta(arrived_slice, arrived_codes, flattened_down, flattened_up, owner_totals):
    source_count = arrived_codes.shape[0]
    item_count = arrived_codes.shape[1]
    down_map_width = flattened_down.shape[1]
    value_map_width = flattened_up.shape[1]
    flat_codes = arrived_codes.reshape(-1)
    products = jnp.einsum(
        "sd,ad->sa",
        arrived_slice.reshape(-1, down_map_width),
        flattened_down,
        preferred_element_type=jnp.float32,
    )
    partial_value = pick_rank(flat_codes, products, owner_totals)
    summed = taken_together(partial_value, "narrow").astype(jnp.bfloat16)
    spread_gradient = spread_rank(flat_codes, summed, owner_totals)
    delta_slots = (
        ADAPTER_SCALE * jnp.dot(spread_gradient, flattened_up, preferred_element_type=jnp.float32)
    ).astype(jnp.bfloat16)
    return lax.all_to_all(
        delta_slots.reshape(source_count, item_count, value_map_width),
        "wide",
        split_axis=0,
        concat_axis=0,
        tiled=True,
    )


def attend(queries, cached_key_rows, cached_value_rows, lengths, fresh_keys, fresh_values):
    row_count = queries.shape[0]
    kv_local = fresh_keys.shape[1] // HEAD_SIZE
    group = HEADS // KEY_VALUE_HEADS
    query_heads = queries.reshape(row_count, kv_local, group, HEAD_SIZE)
    key_heads = cached_key_rows.reshape(row_count, CACHE, kv_local, HEAD_SIZE)
    value_heads = cached_value_rows.reshape(row_count, CACHE, kv_local, HEAD_SIZE)
    inverse = 1.0 / math.sqrt(HEAD_SIZE)
    scores = (
        jnp.einsum("bhgd,bphd->bhgp", query_heads, key_heads, preferred_element_type=jnp.float32)
        * inverse
    )
    own_score = (
        jnp.einsum(
            "bhgd,bhd->bhg",
            query_heads,
            fresh_keys.reshape(row_count, kv_local, HEAD_SIZE),
            preferred_element_type=jnp.float32,
        )
        * inverse
    )
    allowed = jnp.arange(CACHE, dtype=jnp.int32)[None, :] < lengths[:, None]
    scores = jnp.where(allowed[:, None, None, :], scores, NEG_FILL)
    highest = jnp.maximum(jnp.max(scores, axis=-1), own_score)
    cache_exp = jnp.exp(scores - highest[..., None])
    own_exp = jnp.exp(own_score - highest)
    denominator = jnp.sum(cache_exp, axis=-1) + own_exp
    cache_weight = (cache_exp / denominator[..., None]).astype(jnp.bfloat16)
    own_weight = (own_exp / denominator).astype(jnp.bfloat16)
    attended = jnp.einsum(
        "bhgp,bphd->bhgd", cache_weight, value_heads, preferred_element_type=jnp.float32
    )
    attended = attended + own_weight.astype(jnp.float32)[..., None] * fresh_values.reshape(
        row_count, kv_local, 1, HEAD_SIZE
    ).astype(jnp.float32)
    return attended.reshape(row_count, -1).astype(jnp.bfloat16)


def per_device(
    decode_hidden_input,
    queries,
    cached_key_rows,
    cached_value_rows,
    lengths,
    decode_adapter_index,
    key_matrix,
    value_matrix,
    adapter_down_map,
    adapter_up_map,
    training_hidden_input,
    cotangent,
    training_adapter_index,
    rewards,
):
    wide_count = lax.axis_size("wide")
    narrow_index = lax.axis_index("narrow")
    owner_totals = adapter_down_map.shape[0]
    down_map_width = adapter_down_map.shape[2]
    value_map_width = adapter_up_map.shape[2]
    row_count = decode_hidden_input.shape[0]
    token_count = training_hidden_input.shape[0]
    row_capacity = 2 * row_count // wide_count
    token_capacity = 2 * token_count // wide_count
    decode_slice = lax.dynamic_slice_in_dim(
        decode_hidden_input, narrow_index * down_map_width, down_map_width, 1
    )
    fresh_keys = jnp.dot(
        decode_hidden_input, key_matrix, preferred_element_type=jnp.float32
    ).astype(jnp.bfloat16)
    base_values = jnp.dot(decode_hidden_input, value_matrix, preferred_element_type=jnp.float32)
    flattened_down = adapter_down_map.reshape(-1, down_map_width)
    flattened_up = adapter_up_map.reshape(-1, value_map_width)
    decode_match = pack_slots(decode_adapter_index, wide_count, owner_totals, row_capacity)
    decode_codes = place_codes(decode_match, decode_adapter_index % owner_totals + 1, wide_count)
    decode_sent = place_rows(decode_match, decode_slice, wide_count)
    token_match = pack_slots(training_adapter_index, wide_count, owner_totals, token_capacity)
    token_codes = place_codes(token_match, training_adapter_index % owner_totals + 1, wide_count)
    token_rewards = place_codes(token_match, rewards, wide_count)
    sent_rows = place_rows(token_match, training_hidden_input, wide_count)
    sent_grads = place_rows(token_match, cotangent, wide_count)
    arrived_rows, arrived_grads, arrived_codes, received_rewards, arrived_decode, arrived_dcodes = (
        *side_by_side((sent_rows, sent_grads), "wide", 0, 0, 2),
        *side_by_side((token_codes, token_rewards), "wide", 0, 0, 1),
        lax.all_to_all(decode_sent, "wide", split_axis=0, concat_axis=0, tiled=True),
        lax.all_to_all(decode_codes, "wide", split_axis=0, concat_axis=0, tiled=True),
    )
    returned = owner_delta(
        arrived_decode, arrived_dcodes, flattened_down, flattened_up, owner_totals
    )
    value_delta_rows = jnp.einsum(
        "sn,sk->nk",
        decode_match.astype(jnp.bfloat16),
        returned.reshape(-1, value_map_width),
        preferred_element_type=jnp.float32,
    ).astype(jnp.bfloat16)
    fresh_values = (base_values + value_delta_rows.astype(jnp.float32)).astype(jnp.bfloat16)
    attended = attend(
        queries, cached_key_rows, cached_value_rows, lengths, fresh_keys, fresh_values
    )
    flat_rows = arrived_rows.reshape(-1, down_map_width)
    flat_grads = arrived_grads.reshape(-1, value_map_width)
    flat_codes = arrived_codes.reshape(-1)
    part_hidden = pick_rank(
        flat_codes,
        jnp.einsum("sd,ad->sa", flat_rows, flattened_down, preferred_element_type=jnp.float32),
        owner_totals,
    )
    part_back = pick_rank(
        flat_codes,
        jnp.einsum("sk,ak->sa", flat_grads, flattened_up, preferred_element_type=jnp.float32),
        owner_totals,
    )
    hidden_sum, back_sum = (over_pieces(part_hidden, "narrow"), over_pieces(part_back, "narrow"))
    scale_factor = ADAPTER_SCALE * received_rewards.reshape(-1).astype(jnp.float32)[:, None]
    grad_down, grad_up = accumulate(
        flat_codes,
        flat_rows,
        flat_grads,
        (scale_factor * hidden_sum).astype(jnp.bfloat16),
        (scale_factor * back_sum).astype(jnp.bfloat16),
        owner_totals,
    )
    return (attended, fresh_values, grad_down, grad_up)


def solution(mesh):
    return jax.shard_map(
        per_device,
        mesh=mesh,
        in_specs=(
            P("wide", None),
            P("wide", "narrow"),
            P("wide", None, "narrow"),
            P("wide", None, "narrow"),
            P("wide"),
            P("wide"),
            P(None, "narrow"),
            P(None, "narrow"),
            P("wide", None, "narrow"),
            P("wide", None, "narrow"),
            P("wide", "narrow"),
            P("wide", "narrow"),
            P("wide"),
            P("wide"),
        ),
        out_specs=(
            P("wide", "narrow"),
            P("wide", "narrow"),
            P("wide", None, "narrow"),
            P("wide", None, "narrow"),
        ),
        check_vma=False,
    )
```

profile of v0, /device:TPU:6, one launch (start us, length us, event | category | flops | bytes accessed | tf_op | source)
XLA Modules:
  0.0 212.2 jit_solution(15428843151143156340)
XLA Ops:
  8.0 9.0 %reduce-window.6 = s32[32,8,128]{2,1,0:T(8,128)S(1)} reduce-window(s32[32,8,128]{2,1,0:T(8,128)S(1)} %fusion.32, s32[]{:T(128)} %constant.73.clone.1), window={size=1x1x128 pad=0_0x0_0x127_0}, to_apply=%region_7.8 | reduce-window | flops 4161536 | bytes 262148 | tf_op jit(solution)/shard_map/reduce-window
  17.6 3.1 %select_reduce_fusion.1 = (s32[2048]{0:T(1024)S(1)}, s32[2048]{0:T(1024)S(1)}) fusion(s32[1024]{0:T(1024)S(1)} %get-tuple-element.12, s32[1024]{0:T(1024)S(1)} %multiply_add_fusion, s32[1024]{0:T(1024)} %param.27), kind=kLoop, calls=%fused_computation.1 | loop fusion | flops 10481664 | bytes 28672 | tf_op jit(solution)/shard_map/reduce_sum | solution.py:66
  21.5 7.6 %all-to-all-start.4 = ((s32[32,1,128]{2,1,0:T(1,128)}), s32[32,1,128]{2,1,0:T(1,128)S(1)}, u32[]{:S(2)}, u32[]{:S(2)}) async-start(s32[32,1,128]{2,1,0:T(1,128)} %bitcast.10), calls=%async_computation.4 | async-start | bytes 32768 | tf_op jit(solution)/shard_map/all_to_all | solution.py:33
  29.1 2.5 %fusion.5 = bf16[2048,128]{1,0:T(8,128)(2,1)S(1)} fusion(bf16[1024,128]{1,0:T(8,128)(2,1)} %param.25, s32[1024]{0:T(1024)S(1)} %multiply_add_fusion), kind=kOutput, calls=%fused_computation.11 | convolution fusion | flops 539230208 | bytes 790528 | tf_op jit(solution)/shard_map/dot_general | solution.py:59
  31.6 4.7 %fusion.4 = bf16[2048,1024]{1,0:T(8,128)(2,1)S(1)} fusion(bf16[1024,1024]{1,0:T(8,128)(2,1)S(1)} %copy-done, s32[1024]{0:T(1024)S(1)} %multiply_add_fusion), kind=kOutput, calls=%fused_computation.8 | convolution fusion | flops 4299161600 | bytes 6295552 | tf_op jit(solution)/shard_map/dot_general | solution.py:59
  36.3 2.8 %pad_maximum_fusion = bf16[32,64,1152]{2,1,0:T(8,128)(2,1)} fusion(bf16[32,64,128]{2,1,0:T(8,128)(2,1)S(1)} %bitcast.102, bf16[32,64,1024]{2,1,0:T(8,128)(2,1)S(1)} %bitcast.99), kind=kLoop, calls=%fused_computation.5 | loop fusion | flops 9437184 | bytes 9437184 | tf_op jit(solution)/shard_map/concatenate | solution.py:31
  39.1 7.6 %all-to-all-start.5 = ((bf16[32,64,1152]{2,1,0:T(8,128)(2,1)}), bf16[32,64,1152]{2,1,0:T(8,128)(2,1)}, u32[]{:S(2)}, u32[]{:S(2)}) async-start(bf16[32,64,1152]{2,1,0:T(8,128)(2,1)} %pad_maximum_fusion), calls=%async_computation.5 | async-start | bytes 9437184 | tf_op jit(solution)/shard_map/all_to_all | solution.py:33
  48.7 55.7 %all-to-all-done.5 = bf16[32,64,1152]{2,1,0:T(8,128)(2,1)} async-done(((bf16[32,64,1152]{2,1,0:T(8,128)(2,1)}), bf16[32,64,1152]{2,1,0:T(8,128)(2,1)}, u32[]{:S(2)}, u32[]{:S(2)}) %all-to-all-start.5) | async-done | bytes 4718624 | tf_op jit(solution)/shard_map/all_to_all | solution.py:33
  104.4 8.1 %all-to-all-start = ((s32[32,1,2]{2,1,0:T(1,128)}), s32[32,1,2]{2,1,0:T(1,128)}, u32[]{:S(2)}, u32[]{:S(2)}) async-start(s32[32,1,2]{2,1,0:T(1,128)} %bitcast.3), calls=%async_computation | async-start | bytes 32768 | tf_op jit(solution)/shard_map/all_to_all | solution.py:209
  112.5 2.7 %slice.29 = bf16[32,64,1024]{2,1,0:T(8,128)(2,1)S(1)} slice(bf16[32,64,1152]{2,1,0:T(8,128)(2,1)} %all-to-all-done.5), slice={[0:32], [0:64], [0:1024]} | slice | bytes 8388608 | tf_op jit(solution)/shard_map/slice | solution.py:38
  115.2 2.0 copy-done.1
  117.2 2.0 fusion.6
  119.3 2.2 %fusion.15 = bf16[32,128,1]{1,0,2:T(8,128)(2,1)S(1)} fusion(bf16[32,8192]{1,0:T(8,128)(2,1)S(1)} %copy-done.3, bf16[8192,128]{1,0:T(8,128)(2,1)} %param.20), kind=kOutput, calls=%fused_computation.29 | convolution fusion | flops 67112960 | bytes 2629632 | tf_op jit(solution)/shard_map/dot_general | solution.py:191
  124.5 7.4 %all-to-all-start.1 = ((bf16[32,2,1024]{2,1,0:T(2,128)(2,1)}), bf16[32,2,1024]{2,1,0:T(2,128)(2,1)S(1)}, u32[]{:S(2)}, u32[]{:S(2)}) async-start(bf16[32,2,1024]{2,1,0:T(2,128)(2,1)} %reshape.347), calls=%async_computation.1 | async-start | bytes 262144 | tf_op jit(solution)/shard_map/all_to_all | solution.py:208
  132.5 2.0 reduce.7
  140.5 2.0 fusion.7
  144.3 8.5 %all-to-all-start.2 = ((f32[8,1,1024]{2,1,0:T(1,128)}), f32[8,1,1024]{2,1,0:T(1,128)S(1)}, u32[]{:S(2)}, u32[]{:S(2)}) async-start(f32[8,1,1024]{2,1,0:T(1,128)} %reshape.376), calls=%async_computation.2 | async-start | bytes 65536 | tf_op jit(solution)/shard_map/all_to_all | solution.py:20
  153.5 7.3 %all-to-all-done.2 = f32[8,1,1024]{2,1,0:T(1,128)S(1)} async-done(((f32[8,1,1024]{2,1,0:T(1,128)}), f32[8,1,1024]{2,1,0:T(1,128)S(1)}, u32[]{:S(2)}, u32[]{:S(2)}) %all-to-all-start.2) | async-done | bytes 32800 | tf_op jit(solution)/shard_map/all_to_all | solution.py:20
  163.8 6.8 %all-to-all-start.3 = ((bf16[32,2,128]{2,1,0:T(2,128)(2,1)}), bf16[32,2,128]{2,1,0:T(2,128)(2,1)S(1)}, u32[]{:S(2)}, u32[]{:S(2)}) async-start(bf16[32,2,128]{2,1,0:T(2,128)(2,1)} %bitcast.5), calls=%async_computation.3 | async-start | bytes 32768 | tf_op jit(solution)/shard_map/all_to_all | solution.py:116
  171.4 4.6 %all-to-all-done.3 = bf16[32,2,128]{2,1,0:T(2,128)(2,1)S(1)} async-done(((bf16[32,2,128]{2,1,0:T(2,128)(2,1)}), bf16[32,2,128]{2,1,0:T(2,128)(2,1)S(1)}, u32[]{:S(2)}, u32[]{:S(2)}) %all-to-all-start.3) | async-done | bytes 16416 | tf_op jit(solution)/shard_map/all_to_all | solution.py:116
  176.9 2.7 %fusion.51 = (f32[32,128]{1,0:T(8,128)S(1)}, bf16[32,128]{1,0:T(8,128)(2,1)}) fusion(f32[32,128]{1,0:T(8,128)S(1)} %fusion.13, bf16[32,8192]{1,0:T(8,128)(2,1)S(1)} %copy-done.3, bf16[8192,128]{1,0:T(8,128)(2,1)} %param.21), kind=kOutput, calls=%fused_computation.104 | convolution fusion | flops 67121152 | bytes 2662400 | tf_op jit(solution)/shard_map/dot_general | solution.py:194
  182.6 16.9 %all-gather.5.cloned.1.call-done = f32[16384,16]{0,1:T(8,128)} async-done(((f32[2048,16]{0,1:T(8,128)}), f32[16384,16]{0,1:T(8,128)}) %all-gather.5.cloned.1.call-update) | async-done | bytes 1048592 | tf_op jit(solution)/shard_map/all_gather | solution.py:44
  199.4 2.0 copy.33
  202.0 2.2 %fusion.18 = f32[16,16,1024]{2,1,0:T(8,128)} fusion(bf16[2048,1024,1]{1,0,2:T(8,128)(2,1)S(1)} %bitcast.98, bf16[2048,16]{0,1:T(8,128)(2,1)S(1)} %get-tuple-element.11, bf16[2048,16]{0,1:T(8,128)(2,1)S(1)} %copy-done.11), kind=kOutput, calls=%fused_computation.34 | convolution fusion | flops 1074266112 | bytes 5373952 | tf_op jit(solution)/shard_map/sa,sd->ad/dot_general | solution.py:87
  (105 shorter events, 25.6 us)
Async XLA Ops:
  7.2 24.4 %copy-start = (bf16[1024,1024]{1,0:T(8,128)(2,1)S(1)}, bf16[1024,1024]{1,0:T(8,128)(2,1)}, u32[]{:S(2)}) copy-start(bf16[1024,1024]{1,0:T(8,128)(2,1)} %param.24) | copy-start | bytes 6291460
  21.5 17.6 %all-to-all-start.4 = ((s32[32,1,128]{2,1,0:T(1,128)}), s32[32,1,128]{2,1,0:T(1,128)S(1)}, u32[]{:S(2)}, u32[]{:S(2)}) async-start(s32[32,1,128]{2,1,0:T(1,128)} %bitcast.10), calls=%async_computation.4 | async-start | bytes 32768 | tf_op jit(solution)/shard_map/all_to_all | solution.py:33
  39.1 7.6 %copy-start.21 = (s32[32]{0:T(128)S(1)}, s32[32]{0:T(128)}, u32[]{:S(2)}) copy-start(s32[32]{0:T(128)} %param.19) | copy-start | bytes 388
  39.1 8.8 %copy-start.15 = (bf16[32,1024]{1,0:T(8,128)(2,1)S(1)}, bf16[32,1024]{1,0:T(8,128)(2,1)}, u32[]{:S(2)}) copy-start(bf16[32,1024]{1,0:T(8,128)(2,1)} %param.15) | copy-start | bytes 196612
  39.1 8.8 %copy-start.9 = (s32[32,1,128]{2,1,0:T(1,128)}, s32[32,1,128]{2,1,0:T(1,128)S(1)}, u32[]{:S(2)}) copy-start(s32[32,1,128]{2,1,0:T(1,128)S(1)} %all-to-all-done.4) | copy-start | bytes 49156
  39.1 65.2 %all-to-all-start.5 = ((bf16[32,64,1152]{2,1,0:T(8,128)(2,1)}), bf16[32,64,1152]{2,1,0:T(8,128)(2,1)}, u32[]{:S(2)}, u32[]{:S(2)}) async-start(bf16[32,64,1152]{2,1,0:T(8,128)(2,1)} %pad_maximum_fusion), calls=%async_computation.5 | async-start | bytes 9437184 | tf_op jit(solution)/shard_map/all_to_all | solution.py:33
  47.1 68.1 %copy-start.17 = (s32[32]{0:T(128)}, s32[32]{0:T(128)S(1)}, u32[]{:S(2)}) copy-start(s32[32]{0:T(128)S(1)} %multiply_add_fusion.1) | copy-start | bytes 388
  47.9 67.3 %copy-start.16 = (s32[16]{0:T(128)}, s32[16]{0:T(128)S(1)}, u32[]{:S(2)}) copy-start(s32[16]{0:T(128)S(1)} %iota_add_fusion) | copy-start | bytes 196
  48.7 66.5 %copy-start.10 = (f32[2048,16]{0,1:T(8,128)}, f32[2048,16]{0,1:T(8,128)S(1)}, u32[]{:S(2)}) copy-start(f32[2048,16]{0,1:T(8,128)S(1)} %get-tuple-element.9) | copy-start | bytes 393220
  104.4 20.2 %all-to-all-start = ((s32[32,1,2]{2,1,0:T(1,128)}), s32[32,1,2]{2,1,0:T(1,128)}, u32[]{:S(2)}, u32[]{:S(2)}) async-start(s32[32,1,2]{2,1,0:T(1,128)} %bitcast.3), calls=%async_computation | async-start | bytes 32768 | tf_op jit(solution)/shard_map/all_to_all | solution.py:209
  112.4 4.8 %copy-start.5 = (bf16[16,16,1024]{2,1,0:T(8,128)(2,1)S(1)}, bf16[16,16,1024]{2,1,0:T(8,128)(2,1)}, u32[]{:S(2)}) copy-start(bf16[16,16,1024]{2,1,0:T(8,128)(2,1)} %param.22) | copy-start | bytes 1572868
  112.5 68.3 %all-gather.7.cloned.1.call-start = ((), (), s32[]{:S(2)}) async-start(), calls=%async_computation.7 | async-start | bytes 1179648 | tf_op jit(solution)/shard_map/all_gather | solution.py:44
  119.2 2.4 %copy-start.4 = (bf16[32,256,128]{2,1,0:T(8,128)(2,1)S(1)}, bf16[32,256,128]{2,1,0:T(8,128)(2,1)}, u32[]{:S(2)}) copy-start(bf16[32,256,128]{2,1,0:T(8,128)(2,1)} %param.16) | copy-start | bytes 6291460
  119.3 3.1 %copy-start.18 = (s32[32]{0:T(128)S(1)}, s32[32]{0:T(128)}, u32[]{:S(2)}) copy-start(s32[32]{0:T(128)} %copy-done.17) | copy-start | bytes 388
  124.5 13.3 %all-to-all-start.1 = ((bf16[32,2,1024]{2,1,0:T(2,128)(2,1)}), bf16[32,2,1024]{2,1,0:T(2,128)(2,1)S(1)}, u32[]{:S(2)}, u32[]{:S(2)}) async-start(bf16[32,2,1024]{2,1,0:T(2,128)(2,1)} %reshape.347), calls=%async_computation.1 | async-start | bytes 262144 | tf_op jit(solution)/shard_map/all_to_all | solution.py:208
  131.9 67.5 %all-gather.5.cloned.1.call-start = ((), (), s32[]{:S(2)}) async-start(), calls=%async_computation.6 | async-start | bytes 1179648 | tf_op jit(solution)/shard_map/all_gather | solution.py:44
  138.5 4.0 %copy-start.8 = (bf16[64,1024,1]{1,0,2:T(8,128)(2,1)S(1)}, bf16[64,1024,1]{1,0,2:T(8,128)(2,1)}, u32[]{:S(2)}) copy-start(bf16[64,1024,1]{1,0,2:T(8,128)(2,1)} %reshape.362) | copy-start | bytes 393220
  143.5 36.1 %copy-start.13 = (f32[32,8]{1,0:T(8,128)S(1)}, f32[32,8]{1,0:T(8,128)}, u32[]{:S(2)}) copy-start(f32[32,8]{1,0:T(8,128)} %copy-done.12) | copy-start | bytes 3076
  144.3 16.5 %all-to-all-start.2 = ((f32[8,1,1024]{2,1,0:T(1,128)}), f32[8,1,1024]{2,1,0:T(1,128)S(1)}, u32[]{:S(2)}, u32[]{:S(2)}) async-start(f32[8,1,1024]{2,1,0:T(1,128)} %reshape.376), calls=%async_computation.2 | async-start | bytes 65536 | tf_op jit(solution)/shard_map/all_to_all | solution.py:20
  163.8 12.2 %all-to-all-start.3 = ((bf16[32,2,128]{2,1,0:T(2,128)(2,1)}), bf16[32,2,128]{2,1,0:T(2,128)(2,1)S(1)}, u32[]{:S(2)}, u32[]{:S(2)}) async-start(bf16[32,2,128]{2,1,0:T(2,128)(2,1)} %bitcast.5), calls=%async_computation.3 | async-start | bytes 32768 | tf_op jit(solution)/shard_map/all_to_all | solution.py:116
  176.0 3.6 %copy-start.20 = (bf16[32,256,128]{2,1,0:T(8,128)(2,1)S(1)}, bf16[32,256,128]{2,1,0:T(8,128)(2,1)}, u32[]{:S(2)}) copy-start(bf16[32,256,128]{2,1,0:T(8,128)(2,1)} %param.17) | copy-start | bytes 6291460
  199.4 2.5 %copy-start.2 = (bf16[32,64,1024]{2,1,0:T(8,128)(2,1)S(1)}, bf16[32,64,1024]{2,1,0:T(8,128)(2,1)}, u32[]{:S(2)}) copy-start(bf16[32,64,1024]{2,1,0:T(8,128)(2,1)} %copy-done.1) | copy-start | bytes 12582916
  199.4 2.6 %copy-start.11 = (bf16[2048,16]{0,1:T(8,128)(2,1)S(1)}, bf16[2048,16]{0,1:T(8,128)(2,1)}, u32[]{:S(2)}) copy-start(bf16[2048,16]{0,1:T(8,128)(2,1)} %get-tuple-element.8) | copy-start | bytes 196612
  202.0 2.3 %copy-start.7 = (bf16[32,64,128]{2,1,0:T(8,128)(2,1)S(1)}, bf16[32,64,128]{2,1,0:T(8,128)(2,1)}, u32[]{:S(2)}) copy-start(bf16[32,64,128]{2,1,0:T(8,128)(2,1)} %copy-done.6) | copy-start | bytes 1572868
  (6 other events, 8.3 us)
Sparse Core Ops, SparseCore 0:
  119.3 41.2 all-gather.6
  162.4 36.9 all-gather.4
where the time goes:
time: 213 us; the launch traced here: 212 us
  waiting for transfers between devices  85 us (40%)
  starting transfers between devices  46 us (22%)
  other arithmetic  24.8 us (12%)
  matrix products  24.5 us (12%)
  local copies, waits for them, and re-layouts  17.4 us (8%)
  between operations  14.5 us (7%)
    all_to_all x2, waiting for transfers between devices, side_by_side(): lax.all_to_all(both, axis, split_axis=split_dim, concat_axis=concat_dim,...  55.7 us
    all_gather x2, waiting for transfers between devices, over_pieces(): return lax.all_gather(shard, axis).sum(0)  16.9 us
    all_to_all x2, starting transfers between devices, side_by_side(): lax.all_to_all(both, axis, split_axis=split_dim, concat_axis=concat_dim,...  15.2 us
    another operation x3, other arithmetic  9.15 us
    unnamed x51, local copies, waits for them, and re-layouts  8.49 us
    all_to_all x1, starting transfers between devices, copy_for_each(): lax.all_to_all(jnp.broadcast_to(shard[None], (devices, *shard.shape)), ax...  8.46 us
    all_to_all x1, starting transfers between devices, per_device(): lax.all_to_all(decode_codes, 'wide', split_axis=0, concat_axis=0, tiled=T...  8.07 us
    dot_general x3, matrix products, place_rows(): jnp.dot(slot_match.astype(jnp.bfloat16), data, preferred_element_type=jnp...  7.48 us
  transfers between devices with their start and end apart: 8, of which 5 were waited for; matrix products, arithmetic and copies ran while one was open for 20% of the time, Pallas kernels for 0%

commit v1 on v0

v1 whole, which is shorter than its diff:
```python
import functools
import math

import jax
import jax.numpy as jnp
from jax import lax
from jax.experimental import pallas as pl
from jax.experimental.pallas import tpu as pltpu
from jax.sharding import PartitionSpec as P

MESH = pl.DeviceIdType.MESH
F32 = jnp.float32
BF16 = jnp.bfloat16
I32 = jnp.int32

PAIRS = [
    [(1, 0), (0, 1), (3, 0), (0, 3)],
    [(1, 1), (3, 3), (1, 3), (3, 1)],
    [(2, 1), (1, 2), (2, 3), (3, 2)],
    [(2, 0), (0, 2)],
    [(2, 2)],
]
ORDER = [(0, 0, 0), (0, 0, 1)]
for group in PAIRS:
    for flip in (0, 1):
        ORDER += [(dx, dy, flip) for dx, dy in group]

DEV = 32
ZDEV = 8
ROWS = 32
TOK = 1024
FEAT = 1024
VAL = 128
WIDTH = FEAT + VAL
PIECE = WIDTH + 128
HALF = 32
ADP = 16
RANK = 16
AR = ADP * RANK
CACHE = 256
HEAD = 128
GROUP = 8
MODEL = 8192
UNITS = 8


def dot_nt(a, b):
    return lax.dot_general(a, b, (((1,), (1,)), ((), ())), preferred_element_type=F32)


def dot_nn(a, b):
    return lax.dot_general(a, b, (((1,), (0,)), ((), ())), preferred_element_type=F32)


def dot_tn(a, b):
    return lax.dot_general(a, b, (((0,), (0,)), ((), ())), preferred_element_type=F32)


def iota(shape, dim):
    return lax.broadcasted_iota(I32, shape, dim)


def kernel(
    lens, meta, h_h, q_h, k_h, v_h, wk_h, wv_h, d_h, u_h, x_h, c_h,
    att_o, fv_o, gd_o, gu_o,
    xb, hb, hs, qb, kb, vb, wkb, wvb, db, ub,
    send, recv, onehot, dec_s, zs, zr, cr, zds, zdr, rets, retr,
    q32, att32, ow, fk, bv,
    lsem, ssem, rsem, zssem, zrsem, dssem, drsem, bssem, brsem,
):
    w = lax.axis_index("wide")
    n = lax.axis_index("narrow")
    wx, wy, wc = w // 8, (w // 2) % 4, w % 2

    def pick(k, which):
        if isinstance(k, int):
            return ORDER[k][which]
        total = jnp.int32(0)
        for i, o in enumerate(ORDER):
            if o[which]:
                total = jnp.where(k == i, jnp.int32(o[which]), total)
        return total

    def peer(k, sign=1):
        dx, dy, dc = pick(k, 0), pick(k, 1), pick(k, 2)
        px = (wx + 4 + sign * dx) % 4
        py = (wy + 4 + sign * dy) % 4
        return (px * 4 + py) * 2 + (wc + dc) % 2

    loads = [
        (x_h, xb.at[:, pl.ds(0, FEAT)]),
        (c_h, xb.at[:, pl.ds(FEAT, VAL)]),
        (h_h.at[:, pl.ds(pl.multiple_of(n * FEAT, FEAT), FEAT)], hs.at[pl.ds(0, ROWS)]),
        (h_h, hb),
        (q_h, qb),
        (wk_h, wkb),
        (wv_h, wvb),
        (k_h, kb),
        (v_h, vb),
        (d_h, db),
        (u_h, ub),
    ]
    copies = [pltpu.make_async_copy(s, t, lsem.at[i]) for i, (s, t) in enumerate(loads)]
    for cp in copies:
        cp.start()

    barrier = pltpu.get_barrier_semaphore()

    @pl.loop(1, DEV)
    def _(k):
        pl.semaphore_signal(barrier, inc=1, device_id=(peer(k), n), device_id_type=MESH)

    @pl.loop(1, ZDEV)
    def _(z):
        pl.semaphore_signal(barrier, inc=1, device_id=(w, (n + z) % ZDEV), device_id_type=MESH)

    row = meta[...]
    lower = jnp.where(iota((128, 128), 0) < iota((128, 128), 1), 1.0, 0.0).astype(BF16)
    ones = jnp.ones((128, 128), BF16)
    prefix = jnp.concatenate([lower, ones], axis=1)
    idx, rew = row[0:1], row[1:2]
    owner = lax.shift_right_arithmetic(idx, 4)
    code = (idx & 15) + 1
    ids = iota((DEV, 128), 0)
    blocks = [owner[:, 128 * j : 128 * j + 128] == ids for j in range(TOK // 128)]
    hot = [jnp.where(m, 1.0, 0.0) for m in blocks]
    ranks = dot_nn(jnp.concatenate(hot, axis=0).astype(BF16), prefix)
    base = jnp.zeros((DEV, 128), F32)
    keys = []
    for j in range(TOK // 128):
        part = ranks[DEV * j : DEV * j + DEV]
        before = part[:, :128] + base
        keys.append(jnp.sum(hot[j] * before, axis=0, keepdims=True))
        base = base + part[:, 128:]
    key = owner * 64 + jnp.concatenate(keys, axis=1).astype(I32)
    line = iota((16, TOK), 0)
    codef, rewf = code.astype(F32), rew.astype(F32)
    meta_a = jnp.where(line == 0, codef, jnp.where(line == 1, rewf, 0.0)).astype(BF16)
    meta_b = jnp.where(line == 2, codef, jnp.where(line == 3, rewf, 0.0)).astype(BF16)

    didx = row[2:3, :128]
    downer = lax.shift_right_arithmetic(didx, 4)
    dhot = jnp.where(downer == ids, 1.0, 0.0)
    drank = jnp.sum(dhot * dot_nn(dhot.astype(BF16), lower), axis=0, keepdims=True)
    dkey = downer * 2 + drank.astype(I32)
    order_peer = jnp.zeros((DEV, 128), I32)
    for k in range(DEV):
        order_peer = jnp.where(ids == k, peer(k), order_peer)
    dpack = [jnp.where(dkey == order_peer * 2 + d, 1.0, 0.0) for d in range(2)]
    dpack_f = jnp.concatenate(dpack, axis=0)
    dpack_b = dpack_f.astype(BF16)
    dcode = jnp.where(didx >= 0, (didx & 15) + 1, 0).astype(F32)
    dline = jnp.where(iota((16, 128), 0) == 4, dcode, 0.0).astype(BF16)
    dpad = jnp.concatenate([dpack_f, jnp.zeros((64, 128), F32)], axis=0).astype(BF16)
    dmeta = dot_nt(dline, dpad)

    hs[pl.ds(ROWS, 128 - ROWS)] = jnp.zeros((128 - ROWS, FEAT), BF16)
    copies[2].wait()
    picked = dot_nn(dpack_b, hs[...])
    for j in range(8):
        for d in range(2):
            dec_s[pl.ds(d * 8 + j, DEV, stride=16), :] = picked[
                32 * d : 32 * d + 32, 128 * j : 128 * j + 128
            ]
    copies[0].wait()
    copies[1].wait()
    pl.semaphore_wait(barrier, DEV - 1 + ZDEV - 1)

    def copy_a(k, p):
        return pltpu.make_async_remote_copy(
            src_ref=send.at[0, k],
            dst_ref=recv.at[0, k],
            send_sem=ssem.at[0, k],
            recv_sem=rsem.at[0, k],
            device_id=(p, n),
            device_id_type=MESH,
        )

    def copy_b(k, p):
        return pltpu.make_async_remote_copy(
            src_ref=send.at[1, k, :, pl.ds(0, WIDTH)],
            dst_ref=recv.at[1, k, :, pl.ds(0, WIDTH)],
            send_sem=ssem.at[1, k],
            recv_sem=rsem.at[1, k],
            device_id=(p, n),
            device_id_type=MESH,
        )

    lane = iota((16, 128), 1)
    slot = iota((HALF, TOK), 0)

    @pl.loop(0, DEV // 4)
    def _(q):
        peers = [peer(q * 4 + i) for i in range(4)]
        for half in range(2):
            for i in range(4):
                match = (key - (peers[i] * 64 + half * HALF)) == slot
                onehot[half * 128 + i * HALF : half * 128 + i * HALF + HALF, :] = jnp.where(
                    match, 1.0, 0.0
                ).astype(BF16)
        rows = dot_nn(onehot[...], xb[...]).astype(BF16)
        tile = dot_nt(meta_a, onehot[0:128]) + dot_nt(meta_b, onehot[128:256])
        for i in range(4):
            k = q * 4 + i
            mine = jnp.where((lane >= 32 * i) & (lane < 32 * i + 32), tile, 0.0)
            mine = mine + jnp.where((lane == k) | (lane == k + 32), dmeta, 0.0)
            send[0, k, :, 0:WIDTH] = rows[32 * i : 32 * i + 32]
            send[0, k, 0:16, WIDTH:PIECE] = mine.astype(BF16)
            send[0, k, 16:32, WIDTH:PIECE] = dec_s[
                pl.ds(pl.multiple_of(k * 16, 16), 16), :
            ].astype(BF16)
            send[1, k, :, 0:WIDTH] = rows[128 + 32 * i : 128 + 32 * i + 32]
        for i in range(4):
            k = q * 4 + i

            @pl.when(k > 0)
            def _():
                copy_a(k, peers[i]).start()

    @pl.loop(1, DEV)
    def _(k):
        copy_b(k, peer(k)).start()

    recv[0, 0] = send[0, 0]
    recv[1, 0, :, 0:WIDTH] = send[1, 0, :, 0:WIDTH]

    for i in range(3, 11):
        copies[i].wait()

    def project(j, acc):
        at = pl.ds(pl.multiple_of(j * 1024, 1024), 1024)
        part = hb[:, at]
        return acc[0] + dot_nn(part, wkb[at, :]), acc[1] + dot_nn(part, wvb[at, :])

    zero = jnp.zeros((ROWS, 128), F32)
    keys_new, values_new = lax.fori_loop(0, MODEL // 1024, project, (zero, zero))
    fk[...] = keys_new.astype(BF16).astype(F32)
    bv[...] = values_new
    for g in range(GROUP):
        q32[pl.ds(g, ROWS, stride=GROUP), :] = qb[:, 128 * g : 128 * g + 128].astype(F32)
    inverse = 1.0 / math.sqrt(HEAD)
    many = 4

    @pl.loop(0, ROWS // many)
    def _(t):
        scores, owns = [], []
        for i in range(many):
            b = t * many + i
            query = q32[pl.ds(pl.multiple_of(b * 8, 8), 8), :]
            s = dot_nt(query.astype(BF16), kb[b]) * inverse
            allowed = iota((GROUP, CACHE), 1) < lens[b]
            scores.append(jnp.where(allowed, s, -1e30))
            owns.append(jnp.sum(query * fk[pl.ds(b, 1), :], axis=1, keepdims=True) * inverse)
        s = jnp.concatenate(scores, axis=0)
        own = jnp.concatenate(owns, axis=0)
        highest = jnp.maximum(jnp.max(s, axis=1, keepdims=True), own)
        e = jnp.exp(s - highest)
        eo = jnp.exp(own - highest)
        total = jnp.sum(e, axis=1, keepdims=True) + eo
        weight = (e / total).astype(BF16)
        own_weight = (eo / total).astype(BF16).astype(F32)
        at = pl.ds(pl.multiple_of(t * many * 8, many * 8), many * 8)
        ow[at, :] = jnp.broadcast_to(own_weight, (many * 8, 128))
        for i in range(many):
            b = t * many + i
            att32[pl.ds(pl.multiple_of(b * 8, 8), 8), :] = dot_nn(
                weight[8 * i : 8 * i + 8], vb[b]
            )

    gd_o[...] = jnp.zeros_like(gd_o)
    gu_o[...] = jnp.zeros_like(gu_o)

    def copy_z(u, z):
        return pltpu.make_async_remote_copy(
            src_ref=zs.at[u],
            dst_ref=zr.at[u, z],
            send_sem=zssem.at[u, z],
            recv_sem=zrsem.at[u, z],
            device_id=(w, (n + z) % ZDEV),
            device_id_type=MESH,
        )

    def copy_zd(z):
        return pltpu.make_async_remote_copy(
            src_ref=zds,
            dst_ref=zdr.at[z],
            send_sem=dssem.at[z],
            recv_sem=drsem.at[z],
            device_id=(w, (n + z) % ZDEV),
            device_id_type=MESH,
        )

    def copy_back(k, p):
        return pltpu.make_async_remote_copy(
            src_ref=rets.at[k],
            dst_ref=retr.at[k],
            send_sem=bssem.at[k],
            recv_sem=brsem.at[k],
            device_id=(p, n),
            device_id_type=MESH,
        )

    def arrive(u):
        first = (u % 4) * 8

        @pl.loop(0, 8)
        def _(i):
            k = first + i

            @pl.when(k > 0)
            def _():
                @pl.when(u < 4)
                def _():
                    copy_a(k, peer(k)).wait_recv()

                @pl.when(u >= 4)
                def _():
                    copy_b(k, peer(k)).wait_recv()

    def received(u, lo, hi):
        return recv[u // 4, pl.ds((u % 4) * 8, 8), :, lo:hi].reshape(256, hi - lo)

    def choose(codes, products):
        total = jnp.zeros((RANK, products.shape[1]), F32)
        for a in range(ADP):
            total = total + jnp.where(codes == a + 1.0, products[16 * a : 16 * a + 16], 0.0)
        return total

    def spread(codes, factors):
        return jnp.concatenate(
            [jnp.where(codes == a + 1.0, factors, 0.0) for a in range(ADP)], axis=0
        ).astype(BF16)

    def stage_one(u):
        arrive(u)

        @pl.when(u < 4)
        def _():
            tiles = []
            for quad in range(2):
                total = jnp.zeros((16, 128), F32)
                for i in range(4):
                    total = total + recv[0, u * 8 + quad * 4 + i, 0:16, WIDTH:PIECE].astype(F32)
                tiles.append(total)
            both = jnp.concatenate(tiles, axis=1)
            cr[u, 0:2] = both[0:2]
            cr[u + 4, 0:2] = both[2:4]

        codes = cr[u, 0:1]
        hidden = choose(codes, dot_nt(db[...], received(u, 0, FEAT)))
        back = choose(codes, dot_nt(ub[...], received(u, FEAT, WIDTH)))
        zs[u] = jnp.concatenate([hidden, back], axis=0).astype(BF16)

        @pl.loop(1, ZDEV)
        def _(z):
            copy_z(u, z).start()

    def stage_two(u):
        total = zs[u].astype(F32)
        for z in range(1, ZDEV):
            copy_z(u, z).wait_recv()
            total = total + zr[u, z].astype(F32)
        codes = cr[u, 0:1]
        scaled = (2.0 * cr[u, 1:2]) * total
        scaled = scaled.astype(BF16).astype(F32)
        gd_o[...] += dot_nn(spread(codes, scaled[16:32]), received(u, 0, FEAT))
        gu_o[...] += dot_nn(spread(codes, scaled[0:16]), received(u, FEAT, WIDTH))

    def decode_codes():
        def add(k, acc):
            return acc + recv[0, k, 0:16, WIDTH:PIECE].astype(F32)

        total = lax.fori_loop(0, DEV, add, jnp.zeros((16, 128), F32))
        return jnp.where(iota((1, 128), 1) < 64, total[4:5], 0.0)

    def decode_one():
        @pl.loop(0, DEV)
        def _(k):
            dec_s[pl.ds(pl.multiple_of(k * 16, 16), 16), :] = recv[
                0, k, 16:32, WIDTH:PIECE
            ].astype(F32)

        products = jnp.zeros((AR, 128), F32)
        for j in range(8):
            rows = [dec_s[pl.ds(d * 8 + j, DEV, stride=16), :] for d in range(2)]
            rows = jnp.concatenate(rows + [jnp.zeros((64, 128), F32)], axis=0).astype(BF16)
            products = products + dot_nt(db[:, 128 * j : 128 * j + 128], rows)
        zds[...] = choose(decode_codes(), products)

        @pl.loop(1, ZDEV)
        def _(z):
            copy_zd(z).start()

    def decode_two():
        total = zds[...]
        for z in range(1, ZDEV):
            copy_zd(z).wait_recv()
            total = total + zdr[z]
        total = total.astype(BF16).astype(F32)
        delta = 2.0 * dot_tn(spread(decode_codes(), total), ub[...])
        delta = delta.astype(BF16).astype(F32)
        for d in range(2):
            for k in range(DEV):
                rets[k, d : d + 1, :] = delta[32 * d + k : 32 * d + k + 1]

        @pl.loop(1, DEV)
        def _(k):
            copy_back(k, peer(k, -1)).start()

        retr[0] = rets[0]

    rets[...] = jnp.zeros_like(rets)

    @pl.loop(0, UNITS + 1)
    def _(u):
        @pl.when(u < UNITS)
        def _():
            stage_one(u)

        @pl.when(u > 0)
        def _():
            stage_two(u - 1)

        @pl.when(u == 3)
        def _():
            decode_one()

        @pl.when(u == 4)
        def _():
            decode_two()

    @pl.loop(1, DEV)
    def _(k):
        copy_back(k, peer(k, -1)).wait_recv()

    gathered = jnp.zeros((128, 128), F32)
    for d in range(2):
        mine = jnp.concatenate([retr[k, d : d + 1, :] for k in range(DEV)], axis=0)
        gathered = gathered + dot_tn(dpack[d].astype(BF16), mine.astype(BF16))
    fresh = (bv[...] + gathered[0:ROWS]).astype(BF16)
    fv_o[...] = fresh
    fresh = fresh.astype(F32)
    for g in range(GROUP):
        at = pl.ds(g, ROWS, stride=GROUP)
        att_o[:, 128 * g : 128 * g + 128] = (att32[at, :] + ow[at, :] * fresh).astype(BF16)

    @pl.loop(1, DEV)
    def _(k):
        copy_a(k, peer(k)).wait_send()
        copy_b(k, peer(k)).wait_send()
        copy_back(k, peer(k, -1)).wait_send()

    @pl.loop(1, ZDEV)
    def _(z):
        copy_zd(z).wait_send()

        @pl.loop(0, UNITS)
        def _(u):
            copy_z(u, z).wait_send()


def per_device(
    decode_hidden_input,
    queries,
    cached_key_rows,
    cached_value_rows,
    lengths,
    decode_adapter_index,
    key_matrix,
    value_matrix,
    adapter_down_map,
    adapter_up_map,
    training_hidden_input,
    cotangent,
    training_adapter_index,
    rewards,
):
    decode_row = jnp.pad(decode_adapter_index, (0, TOK - ROWS), constant_values=-1)
    meta = jnp.stack([training_adapter_index, rewards, decode_row] + [rewards] * 5)
    vmem = pl.BlockSpec(memory_space=pltpu.VMEM)
    hbm = pl.BlockSpec(memory_space=pl.ANY)
    dma = pltpu.SemaphoreType.DMA
    attended, fresh, down, up = pl.pallas_call(
        kernel,
        out_shape=(
            jax.ShapeDtypeStruct((ROWS, GROUP * HEAD), BF16),
            jax.ShapeDtypeStruct((ROWS, VAL), BF16),
            jax.ShapeDtypeStruct((AR, FEAT), F32),
            jax.ShapeDtypeStruct((AR, VAL), F32),
        ),
        in_specs=[pl.BlockSpec(memory_space=pltpu.SMEM), vmem] + [hbm] * 10,
        out_specs=(vmem,) * 4,
        scratch_shapes=[
            pltpu.VMEM((TOK, WIDTH), BF16),
            pltpu.VMEM((ROWS, MODEL), BF16),
            pltpu.VMEM((128, FEAT), BF16),
            pltpu.VMEM((ROWS, GROUP * HEAD), BF16),
            pltpu.VMEM((ROWS, CACHE, HEAD), BF16),
            pltpu.VMEM((ROWS, CACHE, HEAD), BF16),
            pltpu.VMEM((MODEL, HEAD), BF16),
            pltpu.VMEM((MODEL, HEAD), BF16),
            pltpu.VMEM((AR, FEAT), BF16),
            pltpu.VMEM((AR, VAL), BF16),
            pltpu.VMEM((2, DEV, HALF, PIECE), BF16),
            pltpu.VMEM((2, DEV, HALF, PIECE), BF16),
            pltpu.VMEM((256, TOK), BF16),
            pltpu.VMEM((512, 128), F32),
            pltpu.VMEM((UNITS, 2 * RANK, 256), BF16),
            pltpu.VMEM((UNITS, ZDEV, 2 * RANK, 256), BF16),
            pltpu.VMEM((UNITS, 8, 256), F32),
            pltpu.VMEM((RANK, 128), F32),
            pltpu.VMEM((ZDEV, RANK, 128), F32),
            pltpu.VMEM((DEV, 8, 128), F32),
            pltpu.VMEM((DEV, 8, 128), F32),
            pltpu.VMEM((ROWS * GROUP, HEAD), F32),
            pltpu.VMEM((ROWS * GROUP, HEAD), F32),
            pltpu.VMEM((ROWS * GROUP, HEAD), F32),
            pltpu.VMEM((ROWS, HEAD), F32),
            pltpu.VMEM((ROWS, HEAD), F32),
            dma((11,)),
            dma((2, DEV)),
            dma((2, DEV)),
            dma((UNITS, ZDEV)),
            dma((UNITS, ZDEV)),
            dma((ZDEV,)),
            dma((ZDEV,)),
            dma((DEV,)),
            dma((DEV,)),
        ],
        compiler_params=pltpu.CompilerParams(
            collective_id=0, has_side_effects=True, vmem_limit_bytes=60 << 20
        ),
    )(
        lengths,
        meta,
        decode_hidden_input,
        queries,
        cached_key_rows,
        cached_value_rows,
        key_matrix,
        value_matrix,
        adapter_down_map.reshape(AR, FEAT),
        adapter_up_map.reshape(AR, VAL),
        training_hidden_input,
        cotangent,
    )
    return attended, fresh, down.reshape(ADP, RANK, FEAT), up.reshape(ADP, RANK, VAL)


def solution(mesh):
    return jax.shard_map(
        per_device,
        mesh=mesh,
        in_specs=(
            P("wide", None),
            P("wide", "narrow"),
            P("wide", None, "narrow"),
            P("wide", None, "narrow"),
            P("wide"),
            P("wide"),
            P(None, "narrow"),
            P(None, "narrow"),
            P("wide", None, "narrow"),
            P("wide", None, "narrow"),
            P("wide", "narrow"),
            P("wide", "narrow"),
            P("wide"),
            P("wide"),
        ),
        out_specs=(
            P("wide", "narrow"),
            P("wide", "narrow"),
            P("wide", None, "narrow"),
            P("wide", None, "narrow"),
        ),
        check_vma=False,
    )
```

time: 213 us -> 94.1 us (0.44)
  waiting for transfers between devices: 85 us -> 0 us
  Pallas kernels: 0 us -> 84.9 us
  starting transfers between devices: 46 us -> 0 us
  other arithmetic: 24.8 us -> 0 us
  matrix products: 24.5 us -> 0 us
  between operations: 14.5 us -> 0.65 us
  local copies, waits for them, and re-layouts: 17.4 us -> 8 us
    pallas_call x0 -> x1, Pallas kernels: none -> 84.9 us  [per_device(): pl.pallas_call(kernel, out_shape=(jax.ShapeDtypeStruct((ROWS, GROUP * HEA...]
    all_to_all x6 -> x0, waiting for transfers between devices: 68.1 us -> none  [the longest x2 55.7 us: side_by_side(): lax.all_to_all(both, axis, split_axis=split_dim, concat_axis=concat_dim,...]
    all_to_all x6 -> x0, starting transfers between devices: 45.9 us -> none  [the longest x2 15.2 us: side_by_side(): lax.all_to_all(both, axis, split_axis=split_dim, concat_axis=concat_dim,...]
    dot_general x15 -> x0, matrix products: 24.5 us -> none  [the longest x3 7.48 us: place_rows(): jnp.dot(slot_match.astype(jnp.bfloat16), data, preferred_element_type=jnp...]
    all_gather x2 -> x0, waiting for transfers between devices: 16.9 us -> none  [over_pieces(): return lax.all_gather(shard, axis).sum(0)]
    another operation x4 -> x0, other arithmetic: 9.2 us -> none
    reduce_sum x7 -> x0, other arithmetic: 4.72 us -> none  [the longest x2 3.17 us: place_codes(): jnp.sum(slot_match.astype(jnp.int32) * values[None, :], axis=1)]
    slice x4 -> x0, local copies, waits for them, and re-layouts: 4.02 us -> none  [the longest x2 3.8 us: side_by_side(): gathered.append(lax.slice_in_dim(out, at, at + a.shape[along], axis=along))]
  transfers between devices with their start and end apart: 8 -> 0, of which waited for: 5 -> 0; matrix products, arithmetic and copies ran while one was open for 20% -> 0% of each run, Pallas kernels for 0% -> 0%
where the time goes in v1:
time: 94.1 us; the launch traced here: 93.6 us
  Pallas kernels  84.9 us (90%)
  local copies, waits for them, and re-layouts  8 us (9%)
    pallas_call x1, Pallas kernels, per_device(): pl.pallas_call(kernel, out_shape=(jax.ShapeDtypeStruct((ROWS, GROUP * HEA...  84.9 us
    unnamed x6, local copies, waits for them, and re-layouts  5.77 us

profile of v1, /device:TPU:6, one launch (start us, length us, event | category | flops | bytes accessed | tf_op | source)
XLA Modules:
  0.0 93.6 jit_solution(6354206912414771381)
XLA Ops:
  0.6 0.7 pad.4
  1.3 1.6 %stack.20.meta = s32[8,1024]{1,0:T(8,128)} concatenate(s32[1,1024]{1,0:T(1,128)} %bitcast.18, s32[1,1024]{1,0:T(1,128)} %bitcast.9, s32[1,1024]{1,0:T(1,128)S(1)} %bitcast.17, s32[1,1024]{1,0:T(1,128)} %bitcast.10, s32[1,1024]{1,0:T(1,128)} %bitcast.11, s32[1,1024]{1,0:T(1,128)} %bitcast.12, s32[1,1024]{1,0:T(1,128)} %bitcast.13, s32[1,1024]{1,0:T(1,128)} %bitcast.14), dimensions={0} | concatenate | bytes 65536 | tf_op jit(solution)/shard_map/stack | solution.py:479
  2.9 84.9 %shard_map.165 = (bf16[32,1024]{1,0:T(8,128)(2,1)}, bf16[32,128]{1,0:T(8,128)(2,1)}, f32[256,1024]{1,0:T(8,128)}, f32[256,128]{1,0:T(8,128)}) custom-call(s32[32]{0:T(128)} %lens.1, s32[8,1024]{1,0:T(8,128)} %stack.20.meta, bf16[32,8192]{1,0:T(8,128)(2,1)} %h_h.1, bf16[32,1024]{1,0:T(8,128)(2,1)} %q_h.1, bf16[32,256,128]{2,1,0:T(8,128)(2,1)} %k_h.1, ...), custom_call_target="tpu_custom_call" | custom-call | tf_op jit(solution)/shard_map/pallas_call | solution.py:483
  87.8 0.0 copy-start
  87.8 1.5 %copy.22 = bf16[32,1024]{1,0:T(8,128)(2,1)} copy(bf16[32,1024]{1,0:T(8,128)(2,1)} %get-tuple-element.16) | data formatting | bytes 131072
  89.3 1.3 %copy.23 = bf16[32,128]{1,0:T(8,128)(2,1)} copy(bf16[32,128]{1,0:T(8,128)(2,1)} %get-tuple-element.17) | data formatting | bytes 16384
  90.6 2.3 %copy.24 = f32[16,16,1024]{2,1,0:T(8,128)} copy(f32[16,16,1024]{2,1,0:T(8,128)} %bitcast.7) | data formatting | bytes 2097152
  92.9 0.0 copy-done
  92.9 0.7 copy.25
Async XLA Ops:
  87.8 5.1 %copy-start = (f32[256,128]{1,0:T(8,128)S(1)}, f32[256,128]{1,0:T(8,128)}, u32[]{:S(2)}) copy-start(f32[256,128]{1,0:T(8,128)} %get-tuple-element.11) | copy-start | bytes 393220

commit v2 on v1

--- a/solution.py
+++ b/solution.py
@@ -32,7 +32,8 @@
 FEAT = 1024
 VAL = 128
 WIDTH = FEAT + VAL
-PIECE = WIDTH + 128
+EXTRA = WIDTH + VAL
+PIECE = EXTRA + 128
 HALF = 32
 ADP = 16
 RANK = 16
@@ -41,7 +42,7 @@
 HEAD = 128
 GROUP = 8
 MODEL = 8192
-UNITS = 8
+UNITS = 4
 
 
 def dot_nt(a, b):
@@ -61,10 +62,10 @@
 
 
 def kernel(
-    lens, meta, h_h, q_h, k_h, v_h, wk_h, wv_h, d_h, u_h, x_h, c_h,
+    lens_h, idx_h, rew_h, didx_h, h_h, q_h, k_h, v_h, wk_h, wv_h, d_h, u_h, x_h, c_h,
     att_o, fv_o, gd_o, gu_o,
-    xb, hb, hs, qb, kb, vb, wkb, wvb, db, ub,
-    send, recv, onehot, dec_s, zs, zr, cr, zds, zdr, rets, retr,
+    lens, idxb, rewb, didxb, xb, hb, hs, qb, kb, vb, wkb, wvb, db, ub,
+    send, recv, onehot, dec_s, zsa, zsb, zra, zrb, cr, later, zds, zdr, rets, retr,
     q32, att32, ow, fk, bv,
     lsem, ssem, rsem, zssem, zrsem, dssem, drsem, bssem, brsem,
 ):
@@ -88,6 +89,10 @@
         return (px * 4 + py) * 2 + (wc + dc) % 2
 
     loads = [
+        (idx_h, idxb),
+        (rew_h, rewb),
+        (didx_h, didxb),
+        (lens_h, lens),
         (x_h, xb.at[:, pl.ds(0, FEAT)]),
         (c_h, xb.at[:, pl.ds(FEAT, VAL)]),
         (h_h.at[:, pl.ds(pl.multiple_of(n * FEAT, FEAT), FEAT)], hs.at[pl.ds(0, ROWS)]),
@@ -101,24 +106,24 @@
         (u_h, ub),
     ]
     copies = [pltpu.make_async_copy(s, t, lsem.at[i]) for i, (s, t) in enumerate(loads)]
-    for cp in copies:
+    for cp in copies[:7]:
         cp.start()
 
     barrier = pltpu.get_barrier_semaphore()
 
-    @pl.loop(1, DEV)
-    def _(k):
+    for k in range(1, DEV):
         pl.semaphore_signal(barrier, inc=1, device_id=(peer(k), n), device_id_type=MESH)
-
-    @pl.loop(1, ZDEV)
-    def _(z):
+    for z in range(1, ZDEV):
         pl.semaphore_signal(barrier, inc=1, device_id=(w, (n + z) % ZDEV), device_id_type=MESH)
 
-    row = meta[...]
+    hs[pl.ds(ROWS, 128 - ROWS)] = jnp.zeros((128 - ROWS, FEAT), BF16)
     lower = jnp.where(iota((128, 128), 0) < iota((128, 128), 1), 1.0, 0.0).astype(BF16)
     ones = jnp.ones((128, 128), BF16)
     prefix = jnp.concatenate([lower, ones], axis=1)
-    idx, rew = row[0:1], row[1:2]
+    for cp in copies[:4]:
+        cp.wait()
+    idx = jnp.concatenate([idxb[j : j + 1, :] for j in range(8)], axis=1)
+    rew = jnp.concatenate([rewb[j : j + 1, :] for j in range(8)], axis=1)
     owner = lax.shift_right_arithmetic(idx, 4)
     code = (idx & 15) + 1
     ids = iota((DEV, 128), 0)
@@ -138,7 +143,7 @@
     meta_a = jnp.where(line == 0, codef, jnp.where(line == 1, rewf, 0.0)).astype(BF16)
     meta_b = jnp.where(line == 2, codef, jnp.where(line == 3, rewf, 0.0)).astype(BF16)
 
-    didx = row[2:3, :128]
+    didx = jnp.concatenate([didxb[...], jnp.full((1, 96), -1, I32)], axis=1)
     downer = lax.shift_right_arithmetic(didx, 4)
     dhot = jnp.where(downer == ids, 1.0, 0.0)
     drank = jnp.sum(dhot * dot_nn(dhot.astype(BF16), lower), axis=0, keepdims=True)
@@ -154,16 +159,17 @@
     dpad = jnp.concatenate([dpack_f, jnp.zeros((64, 128), F32)], axis=0).astype(BF16)
     dmeta = dot_nt(dline, dpad)
 
-    hs[pl.ds(ROWS, 128 - ROWS)] = jnp.zeros((128 - ROWS, FEAT), BF16)
-    copies[2].wait()
+    copies[6].wait()
     picked = dot_nn(dpack_b, hs[...])
     for j in range(8):
         for d in range(2):
             dec_s[pl.ds(d * 8 + j, DEV, stride=16), :] = picked[
                 32 * d : 32 * d + 32, 128 * j : 128 * j + 128
             ]
-    copies[0].wait()
-    copies[1].wait()
+    copies[4].wait()
+    copies[5].wait()
+    for cp in copies[7:]:
+        cp.start()
     pl.semaphore_wait(barrier, DEV - 1 + ZDEV - 1)
 
     def copy_a(k, p):
@@ -178,8 +184,8 @@
 
     def copy_b(k, p):
         return pltpu.make_async_remote_copy(
-            src_ref=send.at[1, k, :, pl.ds(0, WIDTH)],
-            dst_ref=recv.at[1, k, :, pl.ds(0, WIDTH)],
+            src_ref=send.at[1, k, :, pl.ds(0, FEAT)],
+            dst_ref=recv.at[1, k, :, pl.ds(0, FEAT)],
             send_sem=ssem.at[1, k],
             recv_sem=rsem.at[1, k],
             device_id=(p, n),
@@ -205,11 +211,12 @@
             mine = jnp.where((lane >= 32 * i) & (lane < 32 * i + 32), tile, 0.0)
             mine = mine + jnp.where((lane == k) | (lane == k + 32), dmeta, 0.0)
             send[0, k, :, 0:WIDTH] = rows[32 * i : 32 * i + 32]
-            send[0, k, 0:16, WIDTH:PIECE] = mine.astype(BF16)
-            send[0, k, 16:32, WIDTH:PIECE] = dec_s[
+            send[0, k, 0:16, EXTRA:PIECE] = mine.astype(BF16)
+            send[0, k, 16:32, EXTRA:PIECE] = dec_s[
                 pl.ds(pl.multiple_of(k * 16, 16), 16), :
             ].astype(BF16)
-            send[1, k, :, 0:WIDTH] = rows[128 + 32 * i : 128 + 32 * i + 32]
+            send[0, k, :, WIDTH:EXTRA] = rows[128 + 32 * i : 128 + 32 * i + 32, FEAT:]
+            send[1, k, :, 0:FEAT] = rows[128 + 32 * i : 128 + 32 * i + 32, :FEAT]
         for i in range(4):
             k = q * 4 + i
 
@@ -222,9 +229,9 @@
         copy_b(k, peer(k)).start()
 
     recv[0, 0] = send[0, 0]
-    recv[1, 0, :, 0:WIDTH] = send[1, 0, :, 0:WIDTH]
-
-    for i in range(3, 11):
+    recv[1, 0, :, 0:FEAT] = send[1, 0, :, 0:FEAT]
+
+    for i in range(7, 15):
         copies[i].wait()
 
     def project(j, acc):
@@ -270,12 +277,13 @@
     gd_o[...] = jnp.zeros_like(gd_o)
     gu_o[...] = jnp.zeros_like(gu_o)
 
-    def copy_z(u, z):
+    def copy_z(u, z, half):
+        src, dst = ((zsa, zra), (zsb, zrb))[half]
         return pltpu.make_async_remote_copy(
-            src_ref=zs.at[u],
-            dst_ref=zr.at[u, z],
-            send_sem=zssem.at[u, z],
-            recv_sem=zrsem.at[u, z],
+            src_ref=src.at[u],
+            dst_ref=dst.at[u, z],
+            send_sem=zssem.at[half, u, z],
+            recv_sem=zrsem.at[half, u, z],
             device_id=(w, (n + z) % ZDEV),
             device_id_type=MESH,
         )
@@ -292,33 +300,16 @@
 
     def copy_back(k, p):
         return pltpu.make_async_remote_copy(
-            src_ref=rets.at[k],
-            dst_ref=retr.at[k],
+            src_ref=rets.at[pl.ds(pl.multiple_of(k * 8, 8), 8)],
+            dst_ref=retr.at[pl.ds(pl.multiple_of(k * 8, 8), 8)],
             send_sem=bssem.at[k],
             recv_sem=brsem.at[k],
             device_id=(p, n),
             device_id_type=MESH,
         )
 
-    def arrive(u):
-        first = (u % 4) * 8
-
-        @pl.loop(0, 8)
-        def _(i):
-            k = first + i
-
-            @pl.when(k > 0)
-            def _():
-                @pl.when(u < 4)
-                def _():
-                    copy_a(k, peer(k)).wait_recv()
-
-                @pl.when(u >= 4)
-                def _():
-                    copy_b(k, peer(k)).wait_recv()
-
-    def received(u, lo, hi):
-        return recv[u // 4, pl.ds((u % 4) * 8, 8), :, lo:hi].reshape(256, hi - lo)
+    def received(half, u, lo, hi):
+        return recv[half, pl.ds(u * 8, 8), :, lo:hi].reshape(256, hi - lo)
 
     def choose(codes, products):
         total = jnp.zeros((RANK, products.shape[1]), F32)
@@ -331,64 +322,75 @@
             [jnp.where(codes == a + 1.0, factors, 0.0) for a in range(ADP)], axis=0
         ).astype(BF16)
 
-    def stage_one(u):
-        arrive(u)
-
-        @pl.when(u < 4)
-        def _():
-            tiles = []
-            for quad in range(2):
-                total = jnp.zeros((16, 128), F32)
-                for i in range(4):
-                    total = total + recv[0, u * 8 + quad * 4 + i, 0:16, WIDTH:PIECE].astype(F32)
-                tiles.append(total)
-            both = jnp.concatenate(tiles, axis=1)
-            cr[u, 0:2] = both[0:2]
-            cr[u + 4, 0:2] = both[2:4]
-
+    def early_one(u):
+        @pl.loop(0, 8)
+        def _(i):
+            k = u * 8 + i
+
+            @pl.when(k > 0)
+            def _():
+                copy_a(k, 0).wait_recv()
+
+        tiles = []
+        for quad in range(2):
+            part = recv[0, pl.ds(u * 8 + quad * 4, 4), 0:16, EXTRA:PIECE].astype(F32)
+            tiles.append(jnp.sum(part, axis=0))
+        cr[u, 0:4] = jnp.concatenate(tiles, axis=1)[0:4]
+        hidden = choose(cr[u, 0:1], dot_nt(db[...], received(0, u, 0, FEAT)))
+        back = choose(cr[u, 0:1], dot_nt(ub[...], received(0, u, FEAT, WIDTH)))
+        back_late = choose(cr[u, 2:3], dot_nt(ub[...], received(0, u, WIDTH, EXTRA)))
+        zsa[u] = jnp.concatenate([hidden, back, back_late], axis=0).astype(BF16)
+        for z in range(1, ZDEV):
+            copy_z(u, z, 0).start()
+
+    def early_two(u):
+        total = zsa[u].astype(F32)
+        for z in range(1, ZDEV):
+            copy_z(u, z, 0).wait_recv()
+            total = total + zra[u, z].astype(F32)
         codes = cr[u, 0:1]
-        hidden = choose(codes, dot_nt(db[...], received(u, 0, FEAT)))
-        back = choose(codes, dot_nt(ub[...], received(u, FEAT, WIDTH)))
-        zs[u] = jnp.concatenate([hidden, back], axis=0).astype(BF16)
-
-        @pl.loop(1, ZDEV)
-        def _(z):
-            copy_z(u, z).start()
-
-    def stage_two(u):
-        total = zs[u].astype(F32)
+        scaled = ((2.0 * cr[u, 1:2]) * total[0:32]).astype(BF16).astype(F32)
+        later[u] = ((2.0 * cr[u, 3:4]) * total[32:48]).astype(BF16).astype(F32)
+        gd_o[...] += dot_nn(spread(codes, scaled[16:32]), received(0, u, 0, FEAT))
+        gu_o[...] += dot_nn(spread(codes, scaled[0:16]), received(0, u, FEAT, WIDTH))
+
+    def late_one(u):
+        @pl.loop(0, 8)
+        def _(i):
+            k = u * 8 + i
+
+            @pl.when(k > 0)
+            def _():
+                copy_b(k, 0).wait_recv()
+
+        codes = cr[u, 2:3]
+        rows = received(1, u, 0, FEAT)
+        zsb[u] = choose(codes, dot_nt(db[...], rows)).astype(BF16)
         for z in range(1, ZDEV):
-            copy_z(u, z).wait_recv()
-            total = total + zr[u, z].astype(F32)
-        codes = cr[u, 0:1]
-        scaled = (2.0 * cr[u, 1:2]) * total
-        scaled = scaled.astype(BF16).astype(F32)
-        gd_o[...] += dot_nn(spread(codes, scaled[16:32]), received(u, 0, FEAT))
-        gu_o[...] += dot_nn(spread(codes, scaled[0:16]), received(u, FEAT, WIDTH))
+            copy_z(u, z, 1).start()
+        gd_o[...] += dot_nn(spread(codes, later[u]), rows)
+
+    def late_two(u):
+        total = zsb[u].astype(F32)
+        for z in range(1, ZDEV):
+            copy_z(u, z, 1).wait_recv()
+            total = total + zrb[u, z].astype(F32)
+        scaled = ((2.0 * cr[u, 3:4]) * total).astype(BF16).astype(F32)
+        gu_o[...] += dot_nn(spread(cr[u, 2:3], scaled), received(0, u, WIDTH, EXTRA))
 
     def decode_codes():
-        def add(k, acc):
-            return acc + recv[0, k, 0:16, WIDTH:PIECE].astype(F32)
-
-        total = lax.fori_loop(0, DEV, add, jnp.zeros((16, 128), F32))
+        total = jnp.sum(recv[0, :, 0:16, EXTRA:PIECE].astype(F32), axis=0)
         return jnp.where(iota((1, 128), 1) < 64, total[4:5], 0.0)
 
     def decode_one():
-        @pl.loop(0, DEV)
-        def _(k):
-            dec_s[pl.ds(pl.multiple_of(k * 16, 16), 16), :] = recv[
-                0, k, 16:32, WIDTH:PIECE
-            ].astype(F32)
-
+        dec_s[...] = recv[0, :, 16:32, EXTRA:PIECE].astype(F32).reshape(512, 128)
         products = jnp.zeros((AR, 128), F32)
         for j in range(8):
             rows = [dec_s[pl.ds(d * 8 + j, DEV, stride=16), :] for d in range(2)]
             rows = jnp.concatenate(rows + [jnp.zeros((64, 128), F32)], axis=0).astype(BF16)
             products = products + dot_nt(db[:, 128 * j : 128 * j + 128], rows)
         zds[...] = choose(decode_codes(), products)
-
-        @pl.loop(1, ZDEV)
-        def _(z):
+        for z in range(1, ZDEV):
             copy_zd(z).start()
 
     def decode_two():
@@ -400,55 +402,57 @@
         delta = 2.0 * dot_tn(spread(decode_codes(), total), ub[...])
         delta = delta.astype(BF16).astype(F32)
         for d in range(2):
-            for k in range(DEV):
-                rets[k, d : d + 1, :] = delta[32 * d + k : 32 * d + k + 1]
-
+            rets[pl.ds(d, DEV, stride=8), :] = delta[32 * d : 32 * d + 32]
+        for k in range(1, DEV):
+            copy_back(k, peer(k, -1)).start()
+        retr[0:8] = rets[0:8]
+
+    def decode_three():
         @pl.loop(1, DEV)
         def _(k):
-            copy_back(k, peer(k, -1)).start()
-
-        retr[0] = rets[0]
+            copy_back(k, 0).wait_recv()
+
+        gathered = jnp.zeros((128, 128), F32)
+        for d in range(2):
+            mine = retr[pl.ds(d, DEV, stride=8), :].astype(BF16)
+            gathered = gathered + dot_tn(dpack[d].astype(BF16), mine)
+        fresh = (bv[...] + gathered[0:ROWS]).astype(BF16)
+        fv_o[...] = fresh
+        fresh = fresh.astype(F32)
+        for g in range(GROUP):
+            at = pl.ds(g, ROWS, stride=GROUP)
+            att_o[:, 128 * g : 128 * g + 128] = (att32[at, :] + ow[at, :] * fresh).astype(BF16)
 
     rets[...] = jnp.zeros_like(rets)
 
-    @pl.loop(0, UNITS + 1)
+    @pl.loop(0, UNITS)
     def _(u):
-        @pl.when(u < UNITS)
-        def _():
-            stage_one(u)
+        early_one(u)
 
         @pl.when(u > 0)
         def _():
-            stage_two(u - 1)
-
-        @pl.when(u == 3)
+            early_two(u - 1)
+
+    decode_one()
+    early_two(UNITS - 1)
+    decode_two()
+
+    @pl.loop(0, UNITS)
+    def _(u):
+        late_one(u)
+
+        @pl.when(u > 0)
         def _():
-            decode_one()
-
-        @pl.when(u == 4)
-        def _():
-            decode_two()
+            late_two(u - 1)
+
+    decode_three()
+    late_two(UNITS - 1)
 
     @pl.loop(1, DEV)
     def _(k):
-        copy_back(k, peer(k, -1)).wait_recv()
-
-    gathered = jnp.zeros((128, 128), F32)
-    for d in range(2):
-        mine = jnp.concatenate([retr[k, d : d + 1, :] for k in range(DEV)], axis=0)
-        gathered = gathered + dot_tn(dpack[d].astype(BF16), mine.astype(BF16))
-    fresh = (bv[...] + gathered[0:ROWS]).astype(BF16)
-    fv_o[...] = fresh
-    fresh = fresh.astype(F32)
-    for g in range(GROUP):
-        at = pl.ds(g, ROWS, stride=GROUP)
-        att_o[:, 128 * g : 128 * g + 128] = (att32[at, :] + ow[at, :] * fresh).astype(BF16)
-
-    @pl.loop(1, DEV)
-    def _(k):
-        copy_a(k, peer(k)).wait_send()
-        copy_b(k, peer(k)).wait_send()
-        copy_back(k, peer(k, -1)).wait_send()
+        copy_a(k, 0).wait_send()
+        copy_b(k, 0).wait_send()
+        copy_back(k, 0).wait_send()
 
     @pl.loop(1, ZDEV)
     def _(z):
@@ -456,7 +460,17 @@
 
         @pl.loop(0, UNITS)
         def _(u):
-            copy_z(u, z).wait_send()
+            copy_z(u, z, 0).wait_send()
+            copy_z(u, z, 1).wait_send()
+
+
+def hand_over(a, b, c, d, ao, bo, co, do, sem):
+    pairs = [(c, co), (a, ao), (d, do), (b, bo)]
+    copies = [pltpu.make_async_copy(s, t, sem.at[i]) for i, (s, t) in enumerate(pairs)]
+    for cp in copies:
+        cp.start()
+    for cp in copies:
+        cp.wait()
 
 
 def per_device(
@@ -475,12 +489,10 @@
     training_adapter_index,
     rewards,
 ):
-    decode_row = jnp.pad(decode_adapter_index, (0, TOK - ROWS), constant_values=-1)
-    meta = jnp.stack([training_adapter_index, rewards, decode_row] + [rewards] * 5)
     vmem = pl.BlockSpec(memory_space=pltpu.VMEM)
-    hbm = pl.BlockSpec(memory_space=pl.ANY)
+    hbm = pl.BlockSpec(memory_space=pltpu.HBM)
     dma = pltpu.SemaphoreType.DMA
-    attended, fresh, down, up = pl.pallas_call(
+    results = pl.pallas_call(
         kernel,
         out_shape=(
             jax.ShapeDtypeStruct((ROWS, GROUP * HEAD), BF16),
@@ -488,9 +500,13 @@
             jax.ShapeDtypeStruct((AR, FEAT), F32),
             jax.ShapeDtypeStruct((AR, VAL), F32),
         ),
-        in_specs=[pl.BlockSpec(memory_space=pltpu.SMEM), vmem] + [hbm] * 10,
+        in_specs=[hbm] * 14,
         out_specs=(vmem,) * 4,
         scratch_shapes=[
+            pltpu.SMEM((ROWS,), I32),
+            pltpu.VMEM((8, 128), I32),
+            pltpu.VMEM((8, 128), I32),
+            pltpu.VMEM((1, ROWS), I32),
             pltpu.VMEM((TOK, WIDTH), BF16),
             pltpu.VMEM((ROWS, MODEL), BF16),
             pltpu.VMEM((128, FEAT), BF16),
@@ -505,34 +521,39 @@
             pltpu.VMEM((2, DEV, HALF, PIECE), BF16),
             pltpu.VMEM((256, TOK), BF16),
             pltpu.VMEM((512, 128), F32),
-            pltpu.VMEM((UNITS, 2 * RANK, 256), BF16),
-            pltpu.VMEM((UNITS, ZDEV, 2 * RANK, 256), BF16),
+            pltpu.VMEM((UNITS, 3 * RANK, 256), BF16),
+            pltpu.VMEM((UNITS, RANK, 256), BF16),
+            pltpu.VMEM((UNITS, ZDEV, 3 * RANK, 256), BF16),
+            pltpu.VMEM((UNITS, ZDEV, RANK, 256), BF16),
             pltpu.VMEM((UNITS, 8, 256), F32),
+            pltpu.VMEM((UNITS, RANK, 256), F32),
             pltpu.VMEM((RANK, 128), F32),
             pltpu.VMEM((ZDEV, RANK, 128), F32),
-            pltpu.VMEM((DEV, 8, 128), F32),
-            pltpu.VMEM((DEV, 8, 128), F32),
+            pltpu.VMEM((DEV * 8, 128), F32),
+            pltpu.VMEM((DEV * 8, 128), F32),
             pltpu.VMEM((ROWS * GROUP, HEAD), F32),
             pltpu.VMEM((ROWS * GROUP, HEAD), F32),
             pltpu.VMEM((ROWS * GROUP, HEAD), F32),
             pltpu.VMEM((ROWS, HEAD), F32),
             pltpu.VMEM((ROWS, HEAD), F32),
-            dma((11,)),
+            dma((15,)),
             dma((2, DEV)),
             dma((2, DEV)),
-            dma((UNITS, ZDEV)),
-            dma((UNITS, ZDEV)),
+            dma((2, UNITS, ZDEV)),
+            dma((2, UNITS, ZDEV)),
             dma((ZDEV,)),
             dma((ZDEV,)),
             dma((DEV,)),
             dma((DEV,)),
         ],
         compiler_params=pltpu.CompilerParams(
-            collective_id=0, has_side_effects=True, vmem_limit_bytes=60 << 20
+            collective_id=0, has_side_effects=True, vmem_limit_bytes=34 << 20
         ),
-    )(
+    )(*[pltpu.with_memory_space_constraint(a, pltpu.HBM) for a in (
         lengths,
-        meta,
+        training_adapter_index.reshape(8, 128),
+        rewards.reshape(8, 128),
+        decode_adapter_index.reshape(1, ROWS),
         decode_hidden_input,
         queries,
         cached_key_rows,
@@ -543,7 +564,15 @@
         adapter_up_map.reshape(AR, VAL),
         training_hidden_input,
         cotangent,
-    )
+    )])
+    attended, fresh, down, up = pl.pallas_call(
+        hand_over,
+        out_shape=[jax.ShapeDtypeStruct(r.shape, r.dtype) for r in results],
+        in_specs=[vmem] * 4,
+        out_specs=[hbm] * 4,
+        scratch_shapes=[dma((4,))],
+        compiler_params=pltpu.CompilerParams(vmem_limit_bytes=4 << 20),
+    )(*results)
     return attended, fresh, down.reshape(ADP, RANK, FEAT), up.reshape(ADP, RANK, VAL)
 
 

time: 94.1 us -> 81.6 us (0.87)
  local copies, waits for them, and re-layouts: 8 us -> 0 us
  Pallas kernels: 84.9 us -> 79.5 us
    pallas_call x1, Pallas kernels: 84.9 us -> 78.4 us  [per_device(): pl.pallas_call(kernel, out_shape=(jax.ShapeDtypeStruct((ROWS, GROUP * HEA...]
    unnamed x6 -> x0, local copies, waits for them, and re-layouts: 5.77 us -> none
    another operation x1 -> x0, local copies, waits for them, and re-layouts: 1.57 us -> none  [per_device(): jnp.stack([training_adapter_index, rewards, decode_row] + [rewards] * 5)]
    pallas_call x0 -> x1, Pallas kernels: none -> 1.06 us  [per_device(): pl.pallas_call(hand_over, out_shape=[jax.ShapeDtypeStruct(r.shape, r.dtyp...]
where the time goes in v2:
time: 81.6 us; the launch traced here: 80.1 us
  Pallas kernels  79.5 us (97%)
    pallas_call x1, Pallas kernels, per_device(): pl.pallas_call(kernel, out_shape=(jax.ShapeDtypeStruct((ROWS, GROUP * HEA...  78.4 us

profile of v2, /device:TPU:6, one launch (start us, length us, event | category | flops | bytes accessed | tf_op | source)
XLA Modules:
  0.0 80.1 jit_solution(7214136354523127627)
XLA Ops:
  0.6 78.4 %shard_map.165 = (bf16[32,1024]{1,0:T(8,128)(2,1)S(1)}, bf16[32,128]{1,0:T(8,128)(2,1)S(1)}, f32[256,1024]{1,0:T(8,128)S(1)}, f32[256,128]{1,0:T(8,128)S(1)}) custom-call(s32[32]{0:T(128)} %lens_h.1, s32[8,128]{1,0:T(8,128)} %bitcast.9, s32[8,128]{1,0:T(8,128)} %bitcast.10, s32[1,32]{1,0:T(1,128)} %bitcast.11, bf16[32,8192]{1,0:T(8,128)(2,1)} %h_h.1, ...), custom_call_target="tpu_custom_call" | custom-call | tf_op jit(solution)/shard_map/pallas_call | solution.py:495
  79.1 1.1 %shard_map.166 = (bf16[32,1024]{1,0:T(8,128)(2,1)}, bf16[32,128]{1,0:T(8,128)(2,1)}, f32[256,1024]{1,0:T(8,128)}, f32[256,128]{1,0:T(8,128)}) custom-call(bf16[32,1024]{1,0:T(8,128)(2,1)S(1)} %get-tuple-element.12.a, bf16[32,128]{1,0:T(8,128)(2,1)S(1)} %get-tuple-element.13.b, f32[256,1024]{1,0:T(8,128)S(1)} %get-tuple-element.14.c, ...), custom_call_target="tpu_custom_call" | custom-call | tf_op jit(solution)/shard_map/pallas_call | solution.py:568
